TPU v7x, 256 devices: a whole 4x4x8 slice. The times are simulated.
256 devices in a mesh: dp: 16 (over z, core), tensor: 16 (over x, y).
Axes of the slice: x: 4, y: 4, z: 8, core: 2. Of those that a mesh axis runs over, the one named last changes fastest.
Arguments:
- inputs: bfloat16 [4096, 6144], P('dp'), may hold values from -6 to 6
- grad_hidden: bfloat16 [4096, 24576], P('dp', 'tensor'), may hold values from -6 to 6
- w_blocks: bfloat16 [16, 288, 128, 128], P('tensor', 'dp'), may hold values from -0.15625 to 0.15625
- block_ids: int32 [16, 288], P('tensor', 'dp'), may hold values from 0 to 575, as said below
- counts: int32 [16, 16], P('tensor', 'dp'), may hold values from 1 to 18, 144 in all within a row
Outputs:
- hidden: bfloat16 [4096, 24576], P('dp', 'tensor')
- grad_inputs: bfloat16 [4096, 6144], P('dp', 'tensor')
- grad_blocks: bfloat16 [16, 288, 128, 128], P('tensor', 'dp')
Inputs may be any that keep to these rules, and one draw needn't show every extreme that they name: `block_ids`: within one tensor index all 288 ids are distinct. Each row of counts sums to 144.
All inputs are finite; a program needn't handle non-finite values. No bound on the sum of `counts` on one device may be relied on, other than what follows from the above.
Results may differ from a plain program's by a relative error of at most 0.023.
Values may be sent and summed in bfloat16 or wider, within the bound.
A program may use at most 128 MiB of HBM per device.

v0:
```python
import math
import jax
import jax.numpy as jnp
from jax import lax
from jax.sharding import PartitionSpec as P

GELU_C = 0.7978845608028654
GELU_A = 0.044715


def gelu_value(values):
    inner_arg = GELU_C * (values + GELU_A * values * values * values)
    return 0.5 * values * (1.0 + jnp.tanh(inner_arg))


def gelu_slope(values):
    inner_arg = GELU_C * (values + GELU_A * values * values * values)
    tanh_value = jnp.tanh(inner_arg)
    return 0.5 * (1.0 + tanh_value) + 0.5 * values * (1.0 - tanh_value * tanh_value) * GELU_C * (
        1.0 + 3.0 * GELU_A * values * values
    )


def select_live(gathered, capacity, col_blocks):
    blocks = gathered[0][0]
    ids_row = gathered[1][0]
    owner_counts = gathered[2][0]
    slot_total = ids_row.shape[0]
    live_total = slot_total // 2
    slot_index = jnp.arange(slot_total, dtype=jnp.int32)
    is_live = slot_index % capacity < owner_counts[slot_index // capacity]
    live_order = jnp.argsort(jnp.where(is_live, 0, 1).astype(jnp.int32), stable=True)[:live_total]
    live_ids = ids_row[live_order]
    block_size = blocks.shape[-1]
    grouped = (
        blocks[live_order].reshape(live_total // 16, 16, block_size, block_size),
        (live_ids // col_blocks).reshape(live_total // 16, 16),
        (live_ids % col_blocks).reshape(live_total // 16, 16),
    )
    return (grouped, live_order)


def one_hot(indices, length, dtype):
    return (indices[:, None] == jnp.arange(length, dtype=jnp.int32)[None, :]).astype(dtype)


def per_device(inputs, grad_hidden, w_blocks, block_ids, counts):
    tok_rows, model_width = inputs.shape
    block_size = w_blocks.shape[-1]
    row_blocks = model_width // block_size
    capacity = w_blocks.shape[1]
    col_blocks = grad_hidden.shape[1] // block_size
    group_count = lax.axis_size("dp")
    x_blocks = inputs.reshape(tok_rows, row_blocks, block_size)
    gathered = (
        lax.all_gather(w_blocks, "dp", axis=1, tiled=True),
        lax.all_gather(block_ids, "dp", axis=1, tiled=True),
        lax.all_gather(counts, "dp", axis=1, tiled=True),
    )
    forward_pieces, forward_order = select_live(gathered, capacity, col_blocks)

    def pick_rows(rows_here):
        rows_hot = one_hot(rows_here, row_blocks, jnp.bfloat16)
        return jnp.einsum(
            "trb,gr->tgb", x_blocks, rows_hot, preferred_element_type=jnp.float32
        ).astype(jnp.bfloat16)

    def forward_group(running, group_data):
        block_piece, rows_here, cols_here = group_data
        x_rows = pick_rows(rows_here)
        product = jnp.einsum(
            "tgb,gbc->tgc", x_rows, block_piece, preferred_element_type=jnp.float32
        )
        cols_hot = one_hot(cols_here, col_blocks, jnp.float32)
        placed = jnp.einsum("tgc,gk->tkc", product, cols_hot, precision=lax.Precision.HIGHEST)
        return (running + placed, None)

    pre_three, unused = lax.scan(
        forward_group, jnp.zeros((tok_rows, col_blocks, block_size), jnp.float32), forward_pieces
    )
    pre_act = pre_three.reshape(tok_rows, col_blocks * block_size)
    hidden = gelu_value(pre_act).astype(jnp.bfloat16)
    grad_pre = (grad_hidden.astype(jnp.float32) * gelu_slope(pre_act)).astype(jnp.bfloat16)
    grad_three = grad_pre.reshape(tok_rows, col_blocks, block_size)
    backward_pieces, backward_order = (forward_pieces, forward_order)

    def backward_group(running, group_data):
        block_piece, rows_here, cols_here = group_data
        cols_pick = one_hot(cols_here, col_blocks, jnp.bfloat16)
        grad_piece = jnp.einsum(
            "tkc,gk->tgc", grad_three, cols_pick, preferred_element_type=jnp.float32
        ).astype(jnp.bfloat16)
        contrib = jnp.einsum(
            "tgc,gbc->tgb", grad_piece, block_piece, preferred_element_type=jnp.float32
        )
        x_rows = pick_rows(rows_here)
        weight_part = jnp.einsum(
            "tgb,tgc->gbc", x_rows, grad_piece, preferred_element_type=jnp.float32
        )
        rows_place = one_hot(rows_here, row_blocks, jnp.float32)
        placed = jnp.einsum("tgb,gr->trb", contrib, rows_place, precision=lax.Precision.HIGHEST)
        return (running + placed, weight_part)

    input_three, weight_parts = lax.scan(
        backward_group, jnp.zeros((tok_rows, row_blocks, block_size), jnp.float32), backward_pieces
    )
    live_total = backward_order.shape[0]
    weight_parts = weight_parts.reshape(live_total, block_size, block_size)
    grad_inputs = lax.psum_scatter(
        input_three.reshape(tok_rows, model_width).astype(jnp.bfloat16),
        "tensor",
        scatter_dimension=1,
        tiled=True,
    )
    position = (
        jnp.full((capacity * group_count,), -1, jnp.int32)
        .at[backward_order]
        .set(jnp.arange(live_total, dtype=jnp.int32))
    )
    grad_scale = 1.0 / math.sqrt(tok_rows * group_count)
    picked = weight_parts[jnp.maximum(position, 0)]
    summed = lax.psum_scatter(
        jnp.where((position >= 0)[:, None, None], picked, 0.0).astype(jnp.bfloat16),
        "dp",
        scatter_dimension=0,
        tiled=True,
    ).astype(jnp.float32)
    grad_blocks = (summed * grad_scale).astype(jnp.bfloat16)[None]
    return (hidden, grad_inputs, grad_blocks)


def solution(mesh):
    in_specs = (
        P("dp", None),
        P("dp", "tensor"),
        P("tensor", "dp", None, None),
        P("tensor", "dp"),
        P("tensor", "dp"),
    )
    out_specs = (P("dp", "tensor"), P("dp", "tensor"), P("tensor", "dp", None, None))
    return jax.shard_map(
        per_device, mesh=mesh, in_specs=in_specs, out_specs=out_specs, check_vma=False
    )
```

profile of v0, /device:TPU:6, one launch (start us, length us, event | category | flops | bytes accessed | tf_op | source)
XLA Modules:
  0.0 545.4 jit_solution(3201787974582969719)
XLA Ops:
  12.0 16.4 %all-reduce.2 = (s32[288]{0:T(512)S(1)}, s32[16]{0:T(128)S(1)}) all-reduce(s32[288]{0:T(512)S(1)} %bitcast_dynamic-update-slice_fusion.1, s32[16]{0:T(128)S(1)} %bitcast_dynamic-update-slice_fusion), channel_id=1, replica_groups=mesh['dp'=16,'tensor'=16] {'dp'}, use_global_device_ids=true, to_apply=%add | all-reduce | flops 304 | bytes 2432 | tf_op jit(solution)/shard_map/squeeze | solution.py:26
  29.5 4.5 fusion.45
  33.9 5.5 %fusion.44 = s32[288]{0:T(512)S(1)} fusion(pred[288]{0:T(512)(128)(4,1)S(1)} %compare_reduce_fusion, pred[288]{0:T(512)(128)(4,1)S(1)} %compare_reduce_fusion.1, pred[288]{0:T(512)(128)(4,1)S(1)} %compare_reduce_fusion.2, pred[288]{0:T(512)(128)(4,1)S(1)} %compare_reduce_fusion.3, pred[288]{0:T(512)(128)(4,1)S(1)} %compare_reduce_fusion.4, ...), kind=kLoop, calls=%fused_computation.93 | loop fusion | flops 4896 | bytes 4932 | tf_op jit(solution)/shard_map/jit(_where)/select_n | solution.py:32
  39.5 3.8 sort.17
  50.2 23.5 %all-gather.2.cloned.1.call-done = bf16[1,288,128,128]{3,2,0,1:T(8,128)(2,1)} async-done(((bf16[1,18,128,128]{3,2,0,1:T(8,128)(2,1)}), bf16[1,288,128,128]{3,2,0,1:T(8,128)(2,1)}) %all-gather.2.cloned.1.call-update) | async-done | bytes 9437200 | tf_op jit(solution)/shard_map/all_gather | solution.py:56
  73.7 11.2 %gather_fusion.1 = bf16[144,128,128]{2,1,0:T(8,128)(2,1)} fusion(bf16[288,128,128]{2,1,0:T(8,128)(2,1)} %bitcast.149, s32[1024]{0:T(1024)S(1)} %pad_clamp_fusion.1), kind=kCustom, calls=%fused_computation.1 | custom fusion | bytes 9437760 | tf_op jit(solution)/shard_map/gather | solution.py:36
  84.9 101.2 %while.24 = (s32[]{:T(128)}, f32[256,12,128]{2,1,0:T(8,128)}, s32[9,16]{1,0:T(8,128)S(1)}, bf16[9,16,128,128]{3,2,1,0:T(8,128)(2,1)}, s32[9,16]{1,0:T(8,128)S(1)...) while((s32[]{:T(128)}, f32[256,12,128]{2,1,0:T(8,128)}, s32[9,16]{1,0:T(8,128)S(1)}, ...), condition=%wide.region_2.3_spmd.clone, body=%wide.region_1.2_spmd.clone.sunk | while | flops 261358528 | bytes 17302000 | solution.py:78
  88.3 3.1 copy.46
  91.4 4.1 bitcast_add_fusion.4
  99.0 3.1 copy.46
  102.1 4.8 bitcast_add_fusion.4
  110.4 3.1 copy.46
  113.4 4.8 bitcast_add_fusion.4
  121.7 3.1 copy.46
  124.8 4.8 bitcast_add_fusion.4
  133.0 3.1 copy.46
  136.1 4.8 bitcast_add_fusion.4
  144.3 3.1 copy.46
  147.4 4.8 bitcast_add_fusion.4
  155.6 3.1 copy.46
  158.7 4.8 bitcast_add_fusion.4
  166.9 3.1 copy.46
  170.0 4.8 bitcast_add_fusion.4
  178.3 3.1 copy.46
  181.4 4.8 bitcast_add_fusion.4
  188.9 3.9 fusion.38
  195.4 180.7 %while.25 = (s32[]{:T(128)}, f32[256,48,128]{2,1,0:T(8,128)}, bf16[9,16,128,128]{3,2,1,0:T(8,128)(2,1)}, s32[9,16]{1,0:T(8,128)S(1)}, bf16[9,16,128,128]{3,2,1,0...) while((s32[]{:T(128)}, f32[256,48,128]{2,1,0:T(8,128)}, ...), condition=%wide.region_4.5_spmd.clone, body=%wide.region_3.4_spmd.clone.sunk | while | flops 637535936 | bytes 40108668 | solution.py:104
  200.9 3.1 copy.50
  204.0 7.2 %bitcast_add_fusion.5 = f32[256,48,128]{2,1,0:T(8,128)} fusion(f32[256,48,128]{2,1,0:T(8,128)} %get-tuple-element.344, pred[]{:T(512)S(6)} %compare.100, f32[256,16,128]{2,1,0:T(8,128)} %copy.50, s32[16]{0:T(128)S(1)} %get-tuple-element.308), kind=kOutput, calls=%fused_computation.22.clone.1 | convolution fusion | flops 305136384 | bytes 14680129 | tf_op jit(solution)/shard_map/while/body/eval_jaxpr/tgb,gr->trb/dot_general | solution.py:101
  219.3 3.1 copy.50
  222.4 9.0 %bitcast_add_fusion.5 = f32[256,48,128]{2,1,0:T(8,128)} fusion(f32[256,48,128]{2,1,0:T(8,128)} %get-tuple-element.344, pred[]{:T(512)S(6)} %compare.100, f32[256,16,128]{2,1,0:T(8,128)} %copy.50, s32[16]{0:T(128)S(1)} %get-tuple-element.308), kind=kOutput, calls=%fused_computation.22.clone.1 | convolution fusion | flops 305136384 | bytes 14680129 | tf_op jit(solution)/shard_map/while/body/eval_jaxpr/tgb,gr->trb/dot_general | solution.py:101
  239.6 3.1 copy.50
  242.7 9.0 %bitcast_add_fusion.5 = f32[256,48,128]{2,1,0:T(8,128)} fusion(f32[256,48,128]{2,1,0:T(8,128)} %get-tuple-element.344, pred[]{:T(512)S(6)} %compare.100, f32[256,16,128]{2,1,0:T(8,128)} %copy.50, s32[16]{0:T(128)S(1)} %get-tuple-element.308), kind=kOutput, calls=%fused_computation.22.clone.1 | convolution fusion | flops 305136384 | bytes 14680129 | tf_op jit(solution)/shard_map/while/body/eval_jaxpr/tgb,gr->trb/dot_general | solution.py:101
  259.9 3.1 copy.50
  263.0 9.0 %bitcast_add_fusion.5 = f32[256,48,128]{2,1,0:T(8,128)} fusion(f32[256,48,128]{2,1,0:T(8,128)} %get-tuple-element.344, pred[]{:T(512)S(6)} %compare.100, f32[256,16,128]{2,1,0:T(8,128)} %copy.50, s32[16]{0:T(128)S(1)} %get-tuple-element.308), kind=kOutput, calls=%fused_computation.22.clone.1 | convolution fusion | flops 305136384 | bytes 14680129 | tf_op jit(solution)/shard_map/while/body/eval_jaxpr/tgb,gr->trb/dot_general | solution.py:101
  280.2 3.1 copy.50
  283.2 9.0 %bitcast_add_fusion.5 = f32[256,48,128]{2,1,0:T(8,128)} fusion(f32[256,48,128]{2,1,0:T(8,128)} %get-tuple-element.344, pred[]{:T(512)S(6)} %compare.100, f32[256,16,128]{2,1,0:T(8,128)} %copy.50, s32[16]{0:T(128)S(1)} %get-tuple-element.308), kind=kOutput, calls=%fused_computation.22.clone.1 | convolution fusion | flops 305136384 | bytes 14680129 | tf_op jit(solution)/shard_map/while/body/eval_jaxpr/tgb,gr->trb/dot_general | solution.py:101
  300.5 3.1 copy.50
  303.5 9.0 %bitcast_add_fusion.5 = f32[256,48,128]{2,1,0:T(8,128)} fusion(f32[256,48,128]{2,1,0:T(8,128)} %get-tuple-element.344, pred[]{:T(512)S(6)} %compare.100, f32[256,16,128]{2,1,0:T(8,128)} %copy.50, s32[16]{0:T(128)S(1)} %get-tuple-element.308), kind=kOutput, calls=%fused_computation.22.clone.1 | convolution fusion | flops 305136384 | bytes 14680129 | tf_op jit(solution)/shard_map/while/body/eval_jaxpr/tgb,gr->trb/dot_general | solution.py:101
  323.8 9.0 %bitcast_add_fusion.5 = f32[256,48,128]{2,1,0:T(8,128)} fusion(f32[256,48,128]{2,1,0:T(8,128)} %get-tuple-element.344, pred[]{:T(512)S(6)} %compare.100, f32[256,16,128]{2,1,0:T(8,128)} %copy.50, s32[16]{0:T(128)S(1)} %get-tuple-element.308), kind=kOutput, calls=%fused_computation.22.clone.1 | convolution fusion | flops 305136384 | bytes 14680129 | tf_op jit(solution)/shard_map/while/body/eval_jaxpr/tgb,gr->trb/dot_general | solution.py:101
  344.1 9.0 %bitcast_add_fusion.5 = f32[256,48,128]{2,1,0:T(8,128)} fusion(f32[256,48,128]{2,1,0:T(8,128)} %get-tuple-element.344, pred[]{:T(512)S(6)} %compare.100, f32[256,16,128]{2,1,0:T(8,128)} %copy.50, s32[16]{0:T(128)S(1)} %get-tuple-element.308), kind=kOutput, calls=%fused_computation.22.clone.1 | convolution fusion | flops 305136384 | bytes 14680129 | tf_op jit(solution)/shard_map/while/body/eval_jaxpr/tgb,gr->trb/dot_general | solution.py:101
  364.4 9.0 %bitcast_add_fusion.5 = f32[256,48,128]{2,1,0:T(8,128)} fusion(f32[256,48,128]{2,1,0:T(8,128)} %get-tuple-element.344, pred[]{:T(512)S(6)} %compare.100, f32[256,16,128]{2,1,0:T(8,128)} %copy.50, s32[16]{0:T(128)S(1)} %get-tuple-element.308), kind=kOutput, calls=%fused_computation.22.clone.1 | convolution fusion | flops 305136384 | bytes 14680129 | tf_op jit(solution)/shard_map/while/body/eval_jaxpr/tgb,gr->trb/dot_general | solution.py:101
  376.1 3.2 convert_element_type.50
  379.2 3.4 copy.28
  383.8 12.6 %gather_fusion.2 = bf16[288,128,128]{2,1,0:T(8,128)(2,1)} fusion(bf16[144,128,128]{2,1,0:T(8,128)(2,1)} %bitcast.145, s32[1024]{0:T(1024)S(1)} %pad_clamp_fusion), kind=kCustom, calls=%fused_computation.2 | custom fusion | bytes 18875520 | tf_op jit(solution)/shard_map/gather | solution.py:121
  396.4 9.3 %select_convert_fusion = bf16[288,128,128]{2,1,0:T(8,128)(2,1)} fusion(bf16[288,128,128]{2,1,0:T(8,128)(2,1)} %gather_fusion.2, pred[288]{0:T(512)(128)(4,1)S(1)} %broadcast_compare_fusion.1), kind=kLoop, calls=%fused_computation.47 | loop fusion | flops 4718592 | bytes 18874656 | tf_op jit(solution)/shard_map/convert_element_type | solution.py:123
  408.0 53.7 %reduce-scatter.7.cloned.1.call-done = bf16[384,256]{1,0:T(8,128)(2,1)} async-done(((bf16[6144,256]{1,0:T(8,128)(2,1)}), bf16[384,256]{1,0:T(8,128)(2,1)}) %reduce-scatter.7.cloned.1.call-update) | async-done | bytes 196624
  463.5 73.3 %reduce-scatter.5.cloned.1.call-done = bf16[18,128,128]{2,1,0:T(8,128)(2,1)} async-done(((bf16[288,128,128]{2,1,0:T(8,128)(2,1)}), bf16[18,128,128]{2,1,0:T(8,128)(2,1)}) %reduce-scatter.5.cloned.1.call-update) | async-done | bytes 589840 | tf_op jit(solution)/shard_map/reduce_scatter | solution.py:122
  (159 shorter events, 137.4 us)
Async XLA Ops:
  7.2 66.5 %all-gather.2.cloned.1.call-start = ((), (), s32[]{:S(2)}) async-start(), calls=%async_computation.2 | async-start | bytes 10027008 | tf_op jit(solution)/shard_map/all_gather | solution.py:56
  7.9 453.8 %reduce-scatter.7.cloned.1.call-start = ((), (), s32[]{:S(2)}) async-start(), calls=%async_computation.4 | async-start | bytes 3342336
  197.1 1.0 copy-start
  211.2 1.2 copy-start.1
  215.5 1.0 copy-start
  231.4 1.2 copy-start.1
  235.8 1.0 copy-start
  251.7 1.2 copy-start.1
  256.1 1.0 copy-start
  272.0 1.2 copy-start.1
  276.3 1.0 copy-start
  292.3 1.2 copy-start.1
  296.6 1.0 copy-start
  312.6 1.2 copy-start.1
  316.9 1.0 copy-start
  332.9 1.2 copy-start.1
  337.2 1.0 copy-start
  353.1 1.2 copy-start.1
  357.5 1.0 copy-start
  373.4 1.2 copy-start.1
  382.6 154.2 %reduce-scatter.5.cloned.1.call-start = ((), (), s32[]{:S(2)}) async-start(), calls=%async_computation.3 | async-start | bytes 10027008 | tf_op jit(solution)/shard_map/reduce_scatter | solution.py:122
  405.7 1.2 copy-start.2
Sparse Core Ops, SparseCore 0:
  9.8 63.7 all-gather.1
  382.7 78.9 reduce-scatter.6
  464.3 72.4 reduce-scatter.4
where the time goes:
time: 548 us; the launch traced here: 545 us
  matrix products  211 us (39%)
  waiting for transfers between devices  151 us (28%)
  local copies, waits for them, and re-layouts  118 us (22%)
  other arithmetic  32.6 us (6%)
  blocking collectives  16.4 us (3%)
  between operations  15.2 us (3%)
    dot_general x9, matrix products, backward_group(): jnp.einsum('tgb,gr->trb', contrib, rows_place, precision=lax.Precision.HI...  79.4 us
    reduce_scatter x1, waiting for transfers between devices, per_device(): lax.psum_scatter(jnp.where((position >= 0)[:, None, None], picked, 0.0).a...  73.3 us
    unnamed x4, waiting for transfers between devices  54.4 us
    dot_general x9, matrix products, forward_group(): jnp.einsum('tgc,gk->tkc', product, cols_hot, precision=lax.Precision.HIGH...  42.3 us
    transpose x9, local copies, waits for them, and re-layouts, backward_group(): jnp.einsum('tgc,gbc->tgb', grad_piece, block_piece, preferred_element_typ...  27.9 us
    transpose x9, local copies, waits for them, and re-layouts, forward_group(): jnp.einsum('tgb,gbc->tgc', x_rows, block_piece, preferred_element_type=jn...  27.9 us
    dot_general x9, matrix products, forward_group(): jnp.einsum('tgb,gbc->tgc', x_rows, block_piece, preferred_element_type=jn...  25.5 us
    dot_general x9, matrix products, backward_group(): jnp.einsum('tgc,gbc->tgb', grad_piece, block_piece, preferred_element_typ...  25.1 us
  transfers between devices with their start and end apart: 3, of which 3 were waited for; matrix products, arithmetic and copies ran while one was open for 9% of the time, Pallas kernels for 0%

commit v1 on v0

--- a/solution.py
+++ b/solution.py
@@ -6,6 +6,24 @@
 
 GELU_C = 0.7978845608028654
 GELU_A = 0.044715
+
+
+def ring_gather(array, axis, dim):
+    ways, here, lap = (lax.axis_size(axis), lax.axis_index(axis), array.shape[dim])
+    lengths = [n * ways if d == dim else n for d, n in enumerate(array.shape)]
+    full = lax.dynamic_update_slice_in_dim(
+        jnp.zeros(lengths, array.dtype), array, here * lap, axis=dim
+    )
+    going_up = going_down = array
+    for far in range(1, ways // 2 + 1):
+        going_up = lax.ppermute(going_up, axis, [(d, (d + 1) % ways) for d in range(ways)])
+        full = lax.dynamic_update_slice_in_dim(full, going_up, (here - far) % ways * lap, axis=dim)
+        if 2 * far < ways:
+            going_down = lax.ppermute(going_down, axis, [(d, (d - 1) % ways) for d in range(ways)])
+            full = lax.dynamic_update_slice_in_dim(
+                full, going_down, (here + far) % ways * lap, axis=dim
+            )
+    return full
 
 
 def gelu_value(values):
@@ -53,7 +71,7 @@
     group_count = lax.axis_size("dp")
     x_blocks = inputs.reshape(tok_rows, row_blocks, block_size)
     gathered = (
-        lax.all_gather(w_blocks, "dp", axis=1, tiled=True),
+        ring_gather(w_blocks, "dp", 1),
         lax.all_gather(block_ids, "dp", axis=1, tiled=True),
         lax.all_gather(counts, "dp", axis=1, tiled=True),
     )

time: 548 us -> 584 us (1.066)
  starting transfers between devices: 0.12 us -> 23.5 us
  local copies, waits for them, and re-layouts: 118 us -> 140 us
  waiting for transfers between devices: 151 us -> 143 us
    all_gather x1 -> x0, waiting for transfers between devices: 23.5 us -> none  [per_device(): lax.all_gather(w_blocks, 'dp', axis=1, tiled=True)]
    ppermute x0 -> x15, starting transfers between devices: none -> 23.5 us  [the longest x7 23.4 us: ring_gather(): lax.ppermute(going_down, axis, [(d, (d - 1) % ways) for d in range(ways)])]
    dynamic_update_slice x0 -> x16, local copies, waits for them, and re-layouts: none -> 21.5 us  [the longest x8 11.4 us: ring_gather(): lax.dynamic_update_slice_in_dim(full, going_up, (here - far) % ways * lap...]
    ppermute x0 -> x15, waiting for transfers between devices: none -> 17.6 us  [the longest x7 10.9 us: ring_gather(): lax.ppermute(going_down, axis, [(d, (d - 1) % ways) for d in range(ways)])]
    squeeze x0 -> x1, local copies, waits for them, and re-layouts: none -> 6.02 us  [select_live(): blocks = gathered[0][0]]
    unnamed x4 -> x3, waiting for transfers between devices: 54.4 us -> 52.6 us
    unnamed x13 -> x21, local copies, waits for them, and re-layouts: 17.7 us -> 17.6 us
  transfers between devices with their start and end apart: 3 -> 17, of which waited for: 3 -> 10; matrix products, arithmetic and copies ran while one was open for 9% -> 13% of each run, Pallas kernels for 0% -> 0%
where the time goes in v1:
time: 584 us; the launch traced here: 581 us
  matrix products  212 us (36%)
  waiting for transfers between devices  143 us (24%)
  local copies, waits for them, and re-layouts  140 us (24%)
  other arithmetic  32.5 us (6%)
  starting transfers between devices  23.5 us (4%)
  between operations  15.8 us (3%)
  blocking collectives  13.4 us (2%)
    dot_general x9, matrix products, backward_group(): jnp.einsum('tgb,gr->trb', contrib, rows_place, precision=lax.Precision.HI...  80.1 us
    reduce_scatter x1, waiting for transfers between devices, per_device(): lax.psum_scatter(jnp.where((position >= 0)[:, None, None], picked, 0.0).a...  73.1 us
    unnamed x3, waiting for transfers between devices  52.6 us
    dot_general x9, matrix products, forward_group(): jnp.einsum('tgc,gk->tkc', product, cols_hot, precision=lax.Precision.HIGH...  42.3 us
    transpose x9, local copies, waits for them, and re-layouts, forward_group(): jnp.einsum('tgb,gbc->tgc', x_rows, block_piece, preferred_element_type=jn...  27.9 us
    transpose x9, local copies, waits for them, and re-layouts, backward_group(): jnp.einsum('tgc,gbc->tgb', grad_piece, block_piece, preferred_element_typ...  27.9 us
    dot_general x9, matrix products, forward_group(): jnp.einsum('tgb,gbc->tgc', x_rows, block_piece, preferred_element_type=jn...  25.5 us
    dot_general x9, matrix products, backward_group(): jnp.einsum('tgc,gbc->tgb', grad_piece, block_piece, preferred_element_typ...  25.1 us
  transfers between devices with their start and end apart: 17, of which 10 were waited for; matrix products, arithmetic and copies ran while one was open for 13% of the time, Pallas kernels for 0%

profile of v1, /device:TPU:6, one launch (start us, length us, event | category | flops | bytes accessed | tf_op | source)
XLA Modules:
  0.0 581.2 jit_solution(7284132430312332750)
XLA Ops:
  7.2 5.3 collective-permute-start.1
  16.6 13.4 %all-reduce.2 = (s32[288]{0:T(512)S(1)}, s32[16]{0:T(128)S(1)}) all-reduce(s32[288]{0:T(512)S(1)} %bitcast_dynamic-update-slice_fusion.17, s32[16]{0:T(128)S(1)} %bitcast_dynamic-update-slice_fusion.16), channel_id=1, replica_groups=mesh['dp'=16,'tensor'=16] {'dp'}, use_global_device_ids=true, to_apply=%add | all-reduce | flops 304 | bytes 2432 | tf_op jit(solution)/shard_map/squeeze | solution.py:44
  31.0 4.4 fusion.45
  35.4 5.6 fusion.44
  41.1 3.8 sort.17
  49.4 6.0 %squeeze.55 = bf16[288,128,128]{2,1,0:T(8,128)(2,1)} broadcast(bf16[]{:T(256)} %constant.175.clone.1), dimensions={} | broadcast | bytes 9437186 | tf_op jit(solution)/shard_map/squeeze | solution.py:43
  88.3 3.1 collective-permute-start.11
  95.1 3.7 collective-permute-done.11
  98.8 3.1 collective-permute-start.13
  105.6 3.7 collective-permute-done.13
  110.2 4.2 collective-permute-done.14
  115.3 11.2 %gather_fusion.1 = bf16[144,128,128]{2,1,0:T(8,128)(2,1)} fusion(bf16[288,128,128]{2,1,0:T(8,128)(2,1)} %bitcast_dynamic-update-slice_fusion, s32[1024]{0:T(1024)S(1)} %pad_clamp_fusion.1), kind=kCustom, calls=%fused_computation.1 | custom fusion | bytes 9437760 | tf_op jit(solution)/shard_map/gather | solution.py:54
  126.5 101.2 %while.24 = (s32[]{:T(128)}, f32[256,12,128]{2,1,0:T(8,128)}, s32[9,16]{1,0:T(8,128)S(1)}, bf16[9,16,128,128]{3,2,1,0:T(8,128)(2,1)}, s32[9,16]{1,0:T(8,128)S(1)...) while((s32[]{:T(128)}, f32[256,12,128]{2,1,0:T(8,128)}, s32[9,16]{1,0:T(8,128)S(1)}, ...), condition=%wide.region_2.3_spmd.clone, body=%wide.region_1.2_spmd.clone.sunk | while | flops 261358528 | bytes 17302000 | solution.py:96
  130.0 3.1 copy.45
  133.1 4.1 bitcast_add_fusion.4
  140.7 3.1 copy.45
  143.8 4.8 bitcast_add_fusion.4
  152.0 3.1 copy.45
  155.1 4.8 bitcast_add_fusion.4
  163.3 3.1 copy.45
  166.4 4.8 bitcast_add_fusion.4
  174.6 3.1 copy.45
  177.7 4.8 bitcast_add_fusion.4
  185.9 3.1 copy.45
  189.0 4.8 bitcast_add_fusion.4
  200.3 4.8 bitcast_add_fusion.4
  208.6 3.1 copy.45
  211.7 4.8 bitcast_add_fusion.4
  223.0 4.8 bitcast_add_fusion.4
  230.5 3.9 fusion.38
  237.0 175.9 %while.25 = (s32[]{:T(128)}, f32[256,48,128]{2,1,0:T(8,128)}, bf16[9,16,128,128]{3,2,1,0:T(8,128)(2,1)}, s32[9,16]{1,0:T(8,128)S(1)}, bf16[9,16,128,128]{3,2,1,0...) while((s32[]{:T(128)}, f32[256,48,128]{2,1,0:T(8,128)}, ...), condition=%wide.region_4.5_spmd.clone, body=%wide.region_3.4_spmd.clone.sunk | while | flops 637535936 | bytes 40108668 | solution.py:122
  245.6 7.3 %bitcast_add_fusion.5 = f32[256,48,128]{2,1,0:T(8,128)} fusion(f32[256,48,128]{2,1,0:T(8,128)} %get-tuple-element.352, pred[]{:T(512)S(6)} %compare.115, f32[256,16,128]{2,1,0:T(8,128)} %copy.49, s32[16]{0:T(128)S(1)} %get-tuple-element.316), kind=kOutput, calls=%fused_computation.22.clone.1 | convolution fusion | flops 305136384 | bytes 14680129 | tf_op jit(solution)/shard_map/while/body/eval_jaxpr/tgb,gr->trb/dot_general | solution.py:119
  263.5 9.1 %bitcast_add_fusion.5 = f32[256,48,128]{2,1,0:T(8,128)} fusion(f32[256,48,128]{2,1,0:T(8,128)} %get-tuple-element.352, pred[]{:T(512)S(6)} %compare.115, f32[256,16,128]{2,1,0:T(8,128)} %copy.49, s32[16]{0:T(128)S(1)} %get-tuple-element.316), kind=kOutput, calls=%fused_computation.22.clone.1 | convolution fusion | flops 305136384 | bytes 14680129 | tf_op jit(solution)/shard_map/while/body/eval_jaxpr/tgb,gr->trb/dot_general | solution.py:119
  280.2 3.1 copy.49
  283.3 9.1 %bitcast_add_fusion.5 = f32[256,48,128]{2,1,0:T(8,128)} fusion(f32[256,48,128]{2,1,0:T(8,128)} %get-tuple-element.352, pred[]{:T(512)S(6)} %compare.115, f32[256,16,128]{2,1,0:T(8,128)} %copy.49, s32[16]{0:T(128)S(1)} %get-tuple-element.316), kind=kOutput, calls=%fused_computation.22.clone.1 | convolution fusion | flops 305136384 | bytes 14680129 | tf_op jit(solution)/shard_map/while/body/eval_jaxpr/tgb,gr->trb/dot_general | solution.py:119
  303.0 9.1 %bitcast_add_fusion.5 = f32[256,48,128]{2,1,0:T(8,128)} fusion(f32[256,48,128]{2,1,0:T(8,128)} %get-tuple-element.352, pred[]{:T(512)S(6)} %compare.115, f32[256,16,128]{2,1,0:T(8,128)} %copy.49, s32[16]{0:T(128)S(1)} %get-tuple-element.316), kind=kOutput, calls=%fused_computation.22.clone.1 | convolution fusion | flops 305136384 | bytes 14680129 | tf_op jit(solution)/shard_map/while/body/eval_jaxpr/tgb,gr->trb/dot_general | solution.py:119
  322.8 9.1 %bitcast_add_fusion.5 = f32[256,48,128]{2,1,0:T(8,128)} fusion(f32[256,48,128]{2,1,0:T(8,128)} %get-tuple-element.352, pred[]{:T(512)S(6)} %compare.115, f32[256,16,128]{2,1,0:T(8,128)} %copy.49, s32[16]{0:T(128)S(1)} %get-tuple-element.316), kind=kOutput, calls=%fused_computation.22.clone.1 | convolution fusion | flops 305136384 | bytes 14680129 | tf_op jit(solution)/shard_map/while/body/eval_jaxpr/tgb,gr->trb/dot_general | solution.py:119
  342.5 9.1 %bitcast_add_fusion.5 = f32[256,48,128]{2,1,0:T(8,128)} fusion(f32[256,48,128]{2,1,0:T(8,128)} %get-tuple-element.352, pred[]{:T(512)S(6)} %compare.115, f32[256,16,128]{2,1,0:T(8,128)} %copy.49, s32[16]{0:T(128)S(1)} %get-tuple-element.316), kind=kOutput, calls=%fused_computation.22.clone.1 | convolution fusion | flops 305136384 | bytes 14680129 | tf_op jit(solution)/shard_map/while/body/eval_jaxpr/tgb,gr->trb/dot_general | solution.py:119
  362.3 9.1 %bitcast_add_fusion.5 = f32[256,48,128]{2,1,0:T(8,128)} fusion(f32[256,48,128]{2,1,0:T(8,128)} %get-tuple-element.352, pred[]{:T(512)S(6)} %compare.115, f32[256,16,128]{2,1,0:T(8,128)} %copy.49, s32[16]{0:T(128)S(1)} %get-tuple-element.316), kind=kOutput, calls=%fused_computation.22.clone.1 | convolution fusion | flops 305136384 | bytes 14680129 | tf_op jit(solution)/shard_map/while/body/eval_jaxpr/tgb,gr->trb/dot_general | solution.py:119
  379.0 3.1 copy.49
  382.1 9.1 %bitcast_add_fusion.5 = f32[256,48,128]{2,1,0:T(8,128)} fusion(f32[256,48,128]{2,1,0:T(8,128)} %get-tuple-element.352, pred[]{:T(512)S(6)} %compare.115, f32[256,16,128]{2,1,0:T(8,128)} %copy.49, s32[16]{0:T(128)S(1)} %get-tuple-element.316), kind=kOutput, calls=%fused_computation.22.clone.1 | convolution fusion | flops 305136384 | bytes 14680129 | tf_op jit(solution)/shard_map/while/body/eval_jaxpr/tgb,gr->trb/dot_general | solution.py:119
  401.8 9.1 %bitcast_add_fusion.5 = f32[256,48,128]{2,1,0:T(8,128)} fusion(f32[256,48,128]{2,1,0:T(8,128)} %get-tuple-element.352, pred[]{:T(512)S(6)} %compare.115, f32[256,16,128]{2,1,0:T(8,128)} %copy.49, s32[16]{0:T(128)S(1)} %get-tuple-element.316), kind=kOutput, calls=%fused_computation.22.clone.1 | convolution fusion | flops 305136384 | bytes 14680129 | tf_op jit(solution)/shard_map/while/body/eval_jaxpr/tgb,gr->trb/dot_general | solution.py:119
  412.9 3.2 convert_element_type.50
  416.1 3.4 copy.27
  420.7 12.6 %gather_fusion.2 = bf16[288,128,128]{2,1,0:T(8,128)(2,1)} fusion(bf16[144,128,128]{2,1,0:T(8,128)(2,1)} %bitcast.175, s32[1024]{0:T(1024)S(1)} %pad_clamp_fusion), kind=kCustom, calls=%fused_computation.2 | custom fusion | bytes 18875520 | tf_op jit(solution)/shard_map/gather | solution.py:139
  433.3 9.3 %select_convert_fusion = bf16[288,128,128]{2,1,0:T(8,128)(2,1)} fusion(bf16[288,128,128]{2,1,0:T(8,128)(2,1)} %gather_fusion.2, pred[288]{0:T(512)(128)(4,1)S(1)} %broadcast_compare_fusion.1), kind=kLoop, calls=%fused_computation.47 | loop fusion | flops 4718592 | bytes 18874656 | tf_op jit(solution)/shard_map/convert_element_type | solution.py:141
  444.9 52.6 %reduce-scatter.7.cloned.1.call-done = bf16[384,256]{1,0:T(8,128)(2,1)} async-done(((bf16[6144,256]{1,0:T(8,128)(2,1)}), bf16[384,256]{1,0:T(8,128)(2,1)}) %reduce-scatter.7.cloned.1.call-update) | async-done | bytes 196624
  499.2 73.1 %reduce-scatter.5.cloned.1.call-done = bf16[18,128,128]{2,1,0:T(8,128)(2,1)} async-done(((bf16[288,128,128]{2,1,0:T(8,128)(2,1)}), bf16[18,128,128]{2,1,0:T(8,128)(2,1)}) %reduce-scatter.5.cloned.1.call-update) | async-done | bytes 589840 | tf_op jit(solution)/shard_map/reduce_scatter | solution.py:140
  (207 shorter events, 188.9 us)
Async XLA Ops:
  7.2 490.3 %reduce-scatter.7.cloned.1.call-start = ((), (), s32[]{:S(2)}) async-start(), calls=%async_computation.3 | async-start | bytes 3342336
  7.2 22.8 %collective-permute-start = (bf16[1,18,128,128]{3,2,1,0:T(8,128)(2,1)}, bf16[1,18,128,128]{3,2,1,0:T(8,128)(2,1)S(1)}, u32[]{:S(2)}, u32[]{:S(2)}) collective-permute-start(bf16[1,18,128,128]{3,2,1,0:T(8,128)(2,1)} %param.11), channel_id=1, source_target_pairs={{0,16},{16,32},{32,48},{48,64},{64,80},{80,96},{96,112},{112,128},... | collective-permute-start | bytes 1769480 | tf_op jit(solution)/shard_map/ppermute | solution.py:19
  7.2 37.6 %collective-permute-start.1 = (bf16[1,18,128,128]{3,2,1,0:T(8,128)(2,1)}, bf16[1,18,128,128]{3,2,1,0:T(8,128)(2,1)S(1)}, u32[]{:S(2)}, u32[]{:S(2)}) collective-permute-start(bf16[1,18,128,128]{3,2,1,0:T(8,128)(2,1)} %param.11), channel_id=1, source_target_pairs={{0,240},{16,0},{32,16},{48,32},{64,48},{80,64},{96,80},{112,96},{1... | collective-permute-start | bytes 1769480 | tf_op jit(solution)/shard_map/ppermute | solution.py:22
  30.0 25.5 %copy-start.5 = (bf16[1,18,128,128]{3,2,1,0:T(8,128)(2,1)}, bf16[1,18,128,128]{3,2,1,0:T(8,128)(2,1)S(1)}, u32[]{:S(2)}) copy-start(bf16[1,18,128,128]{3,2,1,0:T(8,128)(2,1)S(1)} %collective-permute-done) | copy-start | bytes 1769476
  30.0 19.3 %collective-permute-start.2 = (bf16[1,18,128,128]{3,2,1,0:T(8,128)(2,1)S(1)}, bf16[1,18,128,128]{3,2,1,0:T(8,128)(2,1)S(1)}, u32[]{:S(2)}, u32[]{:S(2)}) collective-permute-start(bf16[1,18,128,128]{3,2,1,0:T(8,128)(2,1)S(1)} %collective-permute-done), channel_id=1, source_target_pairs={{0,16},{16,32},{32,48},{48,64},{64,80},{80,96},{96,112},{112,128},... | collective-permute-start | bytes 1769480 | tf_op jit(solution)/shard_map/ppermute | solution.py:19
  44.9 10.6 %copy-start.4 = (bf16[1,18,128,128]{3,2,1,0:T(8,128)(2,1)}, bf16[1,18,128,128]{3,2,1,0:T(8,128)(2,1)S(1)}, u32[]{:S(2)}) copy-start(bf16[1,18,128,128]{3,2,1,0:T(8,128)(2,1)S(1)} %collective-permute-done.1) | copy-start | bytes 1769476
  44.9 11.4 %collective-permute-start.3 = (bf16[1,18,128,128]{3,2,1,0:T(8,128)(2,1)S(1)}, bf16[1,18,128,128]{3,2,1,0:T(8,128)(2,1)}, u32[]{:S(2)}, u32[]{:S(2)}) collective-permute-start(bf16[1,18,128,128]{3,2,1,0:T(8,128)(2,1)S(1)} %collective-permute-done.1), channel_id=1, source_target_pairs={{0,240},{16,0},{32,16},{48,32},{64,48},{80,64},{96,80},{112,96},{1... | collective-permute-start | bytes 1769480 | tf_op jit(solution)/shard_map/ppermute | solution.py:22
  49.4 6.1 %copy-start.6 = (bf16[1,18,128,128]{3,2,1,0:T(8,128)(2,1)}, bf16[1,18,128,128]{3,2,1,0:T(8,128)(2,1)S(1)}, u32[]{:S(2)}) copy-start(bf16[1,18,128,128]{3,2,1,0:T(8,128)(2,1)S(1)} %collective-permute-done.2) | copy-start | bytes 1769476
  49.4 10.6 %collective-permute-start.4 = (bf16[1,18,128,128]{3,2,1,0:T(8,128)(2,1)S(1)}, bf16[1,18,128,128]{3,2,1,0:T(8,128)(2,1)}, u32[]{:S(2)}, u32[]{:S(2)}) collective-permute-start(bf16[1,18,128,128]{3,2,1,0:T(8,128)(2,1)S(1)} %collective-permute-done.2), channel_id=1, source_target_pairs={{0,16},{16,32},{32,48},{48,64},{64,80},{80,96},{96,112},{112,128},... | collective-permute-start | bytes 1769480 | tf_op jit(solution)/shard_map/ppermute | solution.py:19
  49.4 6.0 %copy-start.3 = (bf16[1,18,128,128]{3,2,1,0:T(8,128)(2,1)S(1)}, bf16[1,18,128,128]{3,2,1,0:T(8,128)(2,1)}, u32[]{:S(2)}) copy-start(bf16[1,18,128,128]{3,2,1,0:T(8,128)(2,1)} %param.11) | copy-start | bytes 1769476
  56.3 10.9 %collective-permute-start.5 = (bf16[1,18,128,128]{3,2,1,0:T(8,128)(2,1)}, bf16[1,18,128,128]{3,2,1,0:T(8,128)(2,1)}, u32[]{:S(2)}, u32[]{:S(2)}) collective-permute-start(bf16[1,18,128,128]{3,2,1,0:T(8,128)(2,1)} %collective-permute-done.3), channel_id=1, source_target_pairs={{0,240},{16,0},{32,16},{48,32},{64,48},{80,64},{96,80},{112,96},{1... | collective-permute-start | bytes 1769480 | tf_op jit(solution)/shard_map/ppermute | solution.py:22
  60.0 12.1 %collective-permute-start.6 = (bf16[1,18,128,128]{3,2,1,0:T(8,128)(2,1)}, bf16[1,18,128,128]{3,2,1,0:T(8,128)(2,1)}, u32[]{:S(2)}, u32[]{:S(2)}) collective-permute-start(bf16[1,18,128,128]{3,2,1,0:T(8,128)(2,1)} %collective-permute-done.4), channel_id=1, source_target_pairs={{0,16},{16,32},{32,48},{48,64},{64,80},{80,96},{96,112},{112,128},... | collective-permute-start | bytes 1769480 | tf_op jit(solution)/shard_map/ppermute | solution.py:19
  67.2 10.7 %collective-permute-start.7 = (bf16[1,18,128,128]{3,2,1,0:T(8,128)(2,1)}, bf16[1,18,128,128]{3,2,1,0:T(8,128)(2,1)S(1)}, u32[]{:S(2)}, u32[]{:S(2)}) collective-permute-start(bf16[1,18,128,128]{3,2,1,0:T(8,128)(2,1)} %collective-permute-done.5), channel_id=1, source_target_pairs={{0,240},{16,0},{32,16},{48,32},{64,48},{80,64},{96,80},{112,96},{1... | collective-permute-start | bytes 1769480 | tf_op jit(solution)/shard_map/ppermute | solution.py:22
  72.1 10.7 %collective-permute-start.8 = (bf16[1,18,128,128]{3,2,1,0:T(8,128)(2,1)}, bf16[1,18,128,128]{3,2,1,0:T(8,128)(2,1)S(1)}, u32[]{:S(2)}, u32[]{:S(2)}) collective-permute-start(bf16[1,18,128,128]{3,2,1,0:T(8,128)(2,1)} %collective-permute-done.6), channel_id=1, source_target_pairs={{0,16},{16,32},{32,48},{48,64},{64,80},{80,96},{96,112},{112,128},... | collective-permute-start | bytes 1769480 | tf_op jit(solution)/shard_map/ppermute | solution.py:19
  77.9 10.4 %collective-permute-start.9 = (bf16[1,18,128,128]{3,2,1,0:T(8,128)(2,1)S(1)}, bf16[1,18,128,128]{3,2,1,0:T(8,128)(2,1)S(1)}, u32[]{:S(2)}, u32[]{:S(2)}) collective-permute-start(bf16[1,18,128,128]{3,2,1,0:T(8,128)(2,1)S(1)} %collective-permute-done.7), channel_id=1, source_target_pairs={{0,240},{16,0},{32,16},{48,32},{64,48},{80,64},{96,80},{112,96},{1... | collective-permute-start | bytes 1769480 | tf_op jit(solution)/shard_map/ppermute | solution.py:22
  82.8 10.5 %collective-permute-start.10 = (bf16[1,18,128,128]{3,2,1,0:T(8,128)(2,1)S(1)}, bf16[1,18,128,128]{3,2,1,0:T(8,128)(2,1)S(1)}, u32[]{:S(2)}, u32[]{:S(2)}) collective-permute-start(bf16[1,18,128,128]{3,2,1,0:T(8,128)(2,1)S(1)} %collective-permute-done.8), channel_id=1, source_target_pairs={{0,16},{16,32},{32,48},{48,64},{64,80},{80,96},{96,112},{112,128},... | collective-permute-start | bytes 1769480 | tf_op jit(solution)/shard_map/ppermute | solution.py:19
  88.3 10.5 %collective-permute-start.11 = (bf16[1,18,128,128]{3,2,1,0:T(8,128)(2,1)S(1)}, bf16[1,18,128,128]{3,2,1,0:T(8,128)(2,1)S(1)}, u32[]{:S(2)}, u32[]{:S(2)}) collective-permute-start(bf16[1,18,128,128]{3,2,1,0:T(8,128)(2,1)S(1)} %collective-permute-done.9), channel_id=1, source_target_pairs={{0,240},{16,0},{32,16},{48,32},{64,48},{80,64},{96,80},{112,96},{1... | collective-permute-start | bytes 1769480 | tf_op jit(solution)/shard_map/ppermute | solution.py:22
  93.4 10.5 %collective-permute-start.12 = (bf16[1,18,128,128]{3,2,1,0:T(8,128)(2,1)S(1)}, bf16[1,18,128,128]{3,2,1,0:T(8,128)(2,1)S(1)}, u32[]{:S(2)}, u32[]{:S(2)}) collective-permute-start(bf16[1,18,128,128]{3,2,1,0:T(8,128)(2,1)S(1)} %collective-permute-done.10), channel_id=1, source_target_pairs={{0,16},{16,32},{32,48},{48,64},{64,80},{80,96},{96,112},{112,128},... | collective-permute-start | bytes 1769480 | tf_op jit(solution)/shard_map/ppermute | solution.py:19
  98.8 10.5 %collective-permute-start.13 = (bf16[1,18,128,128]{3,2,1,0:T(8,128)(2,1)S(1)}, bf16[1,18,128,128]{3,2,1,0:T(8,128)(2,1)S(1)}, u32[]{:S(2)}, u32[]{:S(2)}) collective-permute-start(bf16[1,18,128,128]{3,2,1,0:T(8,128)(2,1)S(1)} %collective-permute-done.11), channel_id=1, source_target_pairs={{0,240},{16,0},{32,16},{48,32},{64,48},{80,64},{96,80},{112,96},{1... | collective-permute-start | bytes 1769480 | tf_op jit(solution)/shard_map/ppermute | solution.py:22
  103.9 10.5 %collective-permute-start.14 = (bf16[1,18,128,128]{3,2,1,0:T(8,128)(2,1)S(1)}, bf16[1,18,128,128]{3,2,1,0:T(8,128)(2,1)S(1)}, u32[]{:S(2)}, u32[]{:S(2)}) collective-permute-start(bf16[1,18,128,128]{3,2,1,0:T(8,128)(2,1)S(1)} %collective-permute-done.12), channel_id=1, source_target_pairs={{0,16},{16,32},{32,48},{48,64},{64,80},{80,96},{96,112},{112,128},... | collective-permute-start | bytes 1769480 | tf_op jit(solution)/shard_map/ppermute | solution.py:19
  238.7 1.0 copy-start
  245.6 7.9 %copy-start.1 = (bf16[256,16,128]{2,1,0:T(8,128)(2,1)S(1)}, bf16[256,16,128]{2,1,0:T(8,128)(2,1)}, u32[]{:S(2)}) copy-start(bf16[256,16,128]{2,1,0:T(8,128)(2,1)} %copy-done) | copy-start | bytes 3145732 | tf_op jit(solution)/shard_map/while
  256.6 1.0 copy-start
  263.5 9.7 %copy-start.1 = (bf16[256,16,128]{2,1,0:T(8,128)(2,1)S(1)}, bf16[256,16,128]{2,1,0:T(8,128)(2,1)}, u32[]{:S(2)}) copy-start(bf16[256,16,128]{2,1,0:T(8,128)(2,1)} %copy-done) | copy-start | bytes 3145732 | tf_op jit(solution)/shard_map/while
  276.4 1.0 copy-start
  283.3 9.7 %copy-start.1 = (bf16[256,16,128]{2,1,0:T(8,128)(2,1)S(1)}, bf16[256,16,128]{2,1,0:T(8,128)(2,1)}, u32[]{:S(2)}) copy-start(bf16[256,16,128]{2,1,0:T(8,128)(2,1)} %copy-done) | copy-start | bytes 3145732 | tf_op jit(solution)/shard_map/while
  296.1 1.0 copy-start
  303.0 9.7 %copy-start.1 = (bf16[256,16,128]{2,1,0:T(8,128)(2,1)S(1)}, bf16[256,16,128]{2,1,0:T(8,128)(2,1)}, u32[]{:S(2)}) copy-start(bf16[256,16,128]{2,1,0:T(8,128)(2,1)} %copy-done) | copy-start | bytes 3145732 | tf_op jit(solution)/shard_map/while
  315.9 1.0 copy-start
  322.8 9.7 %copy-start.1 = (bf16[256,16,128]{2,1,0:T(8,128)(2,1)S(1)}, bf16[256,16,128]{2,1,0:T(8,128)(2,1)}, u32[]{:S(2)}) copy-start(bf16[256,16,128]{2,1,0:T(8,128)(2,1)} %copy-done) | copy-start | bytes 3145732 | tf_op jit(solution)/shard_map/while
  335.6 1.0 copy-start
  342.5 9.7 %copy-start.1 = (bf16[256,16,128]{2,1,0:T(8,128)(2,1)S(1)}, bf16[256,16,128]{2,1,0:T(8,128)(2,1)}, u32[]{:S(2)}) copy-start(bf16[256,16,128]{2,1,0:T(8,128)(2,1)} %copy-done) | copy-start | bytes 3145732 | tf_op jit(solution)/shard_map/while
  355.4 1.0 copy-start
  362.3 9.7 %copy-start.1 = (bf16[256,16,128]{2,1,0:T(8,128)(2,1)S(1)}, bf16[256,16,128]{2,1,0:T(8,128)(2,1)}, u32[]{:S(2)}) copy-start(bf16[256,16,128]{2,1,0:T(8,128)(2,1)} %copy-done) | copy-start | bytes 3145732 | tf_op jit(solution)/shard_map/while
  375.2 1.0 copy-start
  382.1 9.7 %copy-start.1 = (bf16[256,16,128]{2,1,0:T(8,128)(2,1)S(1)}, bf16[256,16,128]{2,1,0:T(8,128)(2,1)}, u32[]{:S(2)}) copy-start(bf16[256,16,128]{2,1,0:T(8,128)(2,1)} %copy-done) | copy-start | bytes 3145732 | tf_op jit(solution)/shard_map/while
  394.9 1.0 copy-start
  401.8 9.7 %copy-start.1 = (bf16[256,16,128]{2,1,0:T(8,128)(2,1)S(1)}, bf16[256,16,128]{2,1,0:T(8,128)(2,1)}, u32[]{:S(2)}) copy-start(bf16[256,16,128]{2,1,0:T(8,128)(2,1)} %copy-done) | copy-start | bytes 3145732 | tf_op jit(solution)/shard_map/while
  419.5 152.8 %reduce-scatter.5.cloned.1.call-start = ((), (), s32[]{:S(2)}) async-start(), calls=%async_computation.2 | async-start | bytes 10027008 | tf_op jit(solution)/shard_map/reduce_scatter | solution.py:140
  442.6 1.1 copy-start.2
Sparse Core Ops, SparseCore 0:
  419.6 77.8 reduce-scatter.6
  500.0 72.2 reduce-scatter.4
